TPU v7x, 32 devices: a whole 2x2x4 slice. The times are simulated.
32 devices in a mesh: pole: 2 (over x), prow: 8 (over z, y), pcol: 2 (over core).
Axes of the slice: x: 2, y: 2, z: 4, core: 2. Of those that a mesh axis runs over, the one named last changes fastest.
Arguments:
- ancestor_inverse: bfloat16 [8192, 4096], P(('pole', 'prow'), 'pcol'), parts along dimension 0, may hold values from -6 to 6
- l_panel: bfloat16 [8192, 1024], P(('pole', 'prow'), 'pcol'), parts along dimension 0, may hold values from -0.125 to 0.125
- diag_inverse: float32 [2048, 256], P(('pole', 'pcol')), parts along dimension 0, may hold values from -6 to 6
- pattern: int32 [4, 8], replicated, may hold values from 0 to 15, as said below
Outputs:
- column_blocks: float32 [8192, 1024], P(('pole', 'prow'), 'pcol'), parts along dimension 0
- diag_blocks: float32 [2048, 256], P(('pole', 'pcol')), parts along dimension 0
There are 2 independent parts, one for each index of `pole`. A program takes and returns all parts, laid end to end along the dimension named above; an argument that names none is the same for every part. Nothing has to cross between parts.
Inputs may be any that keep to these rules, and one draw needn't show every extreme that they name: `pattern`: each row lists 8 different ancestor supernodes in increasing order, and every row lists ancestor 16 - 1.
All inputs are finite; a program needn't handle non-finite values.
Results may differ from a plain program's by a relative error of at most 0.0003.
Values may be sent and summed in bfloat16 or wider, within the bound.
No kernel may reach another device: no remote copies, remote signals or barrier semaphores. Data moves between devices by JAX's collectives and lax.ppermute only.
A program may use at most 128 MiB of HBM per device.

v0:
```python
import jax
import jax.numpy as jnp
from jax import lax
from jax.sharding import PartitionSpec as P

B = 256


def per_device(ancestor_inverse, l_panel, diag_inverse, pattern):
    row_index = lax.axis_index("prow")
    col_index = lax.axis_index("pcol")
    local_tiles = l_panel.shape[0] // B
    local_nodes = l_panel.shape[1] // B
    tile_ids = row_index * local_tiles + jnp.arange(local_tiles, dtype=jnp.int32)
    node_rows = lax.dynamic_slice_in_dim(pattern, col_index * local_nodes, local_nodes, 0)
    member = jnp.any(node_rows[None, :, :] == tile_ids[:, None, None], axis=2)
    panel_mask = member.astype(jnp.float32)[:, None, :, None]
    masked = (
        l_panel.reshape(local_tiles, B, local_nodes, B) * panel_mask.astype(jnp.bfloat16)
    ).reshape(l_panel.shape)
    swapped = lax.all_to_all(masked, "pcol", split_axis=0, concat_axis=1, tiled=True)
    partial_sum = jnp.dot(
        ancestor_inverse,
        lax.all_gather(swapped, "prow", axis=0, tiled=True),
        preferred_element_type=jnp.float32,
    )
    summed = lax.psum_scatter(partial_sum, "pcol", scatter_dimension=1, tiled=True)
    negated = -summed
    diag_terms = jnp.einsum(
        "rkb,rkc->kbc",
        masked.astype(jnp.float32).reshape(-1, local_nodes, B),
        negated.reshape(-1, local_nodes, B),
        precision=lax.Precision.HIGHEST,
    )
    totals = lax.psum(diag_terms, "prow")
    diag_blocks = diag_inverse - totals.reshape(local_nodes * B, B)
    column_blocks = (negated.reshape(local_tiles, B, local_nodes, B) * panel_mask).reshape(
        negated.shape
    )
    return (column_blocks, diag_blocks)


def solution(mesh):
    return jax.shard_map(
        per_device,
        mesh=mesh,
        in_specs=(
            P(("pole", "prow"), "pcol"),
            P(("pole", "prow"), "pcol"),
            P(("pole", "pcol"), None),
            P(),
        ),
        out_specs=(P(("pole", "prow"), "pcol"), P(("pole", "pcol"), None)),
        check_vma=False,
    )
```

profile of v0, /device:TPU:0, one launch (start us, length us, event | category | flops | bytes accessed | tf_op | source)
XLA Modules:
  0.0 193.1 jit_solution(15879236275212393171)
XLA Ops:
  7.2 0.8 constant_dynamic-slice_fusion
  8.1 0.2 compare_reduce_fusion
  8.3 0.3 mul.39
  8.6 0.1 copy.27
  8.7 1.2 mul.41
  9.9 4.2 %all_to_all.19 = bf16[2,256,512]{2,1,0:T(8,128)(2,1)S(1)} all-to-all(bf16[2,256,512]{2,1,0:T(8,128)(2,1)S(1)} %bitcast.30), channel_id=1, replica_groups=mesh['pole'=2,'prow'=8,'pcol'=2] {'pcol'}, dimensions={0} | all-to-all | bytes 1048576 | tf_op jit(solution)/shard_map/all_to_all | solution.py:21
  14.1 1.0 copy.19
  15.1 0.0 reduce-scatter.2.cloned.1.call-start
  15.1 77.5 %all-gather.2.cloned.1.call-done = bf16[2048,1024]{0,1:T(8,128)(2,1)} async-done(((bf16[256,1024]{0,1:T(8,128)(2,1)}), bf16[2048,1024]{0,1:T(8,128)(2,1)}) %all-gather.2.cloned.1.call-update) | async-done | bytes 4194320 | tf_op jit(solution)/shard_map/all_gather | solution.py:24
  92.6 5.9 %convolution_bitcast_fusion = f32[512,1024]{0,1:T(8,128)} fusion(bf16[2048,1024]{0,1:T(8,128)(2,1)} %all-gather.2.cloned.1.call-done, bf16[512,2048]{1,0:T(8,128)(2,1)S(1)} %copy-done), kind=kOutput, calls=%fused_computation | convolution fusion | flops 2147483648 | bytes 8388608 | tf_op jit(solution)/shard_map/dot_general | solution.py:22
  98.5 0.0 all-reduce.2.cloned.1.call-start
  98.6 0.1 copy.21
  98.7 0.9 copy-done.1
  99.5 1.0 copy.26
  100.5 0.1 copy.20
  100.6 0.3 mul.42
  101.0 1.0 copy.28
  102.0 0.1 broadcast_bitcast_fusion
  102.1 4.5 %reduce-scatter.2.cloned.1.call-done = f32[512,512]{0,1:T(8,128)} async-done(((f32[512,1024]{0,1:T(8,128)}), f32[512,512]{0,1:T(8,128)}) %reduce-scatter.2.cloned.1.call-update) | async-done | bytes 1048592 | tf_op jit(solution)/shard_map/reduce_scatter | solution.py:27
  106.6 1.8 fusion.3
  108.5 1.5 fusion
  110.0 1.3 copy.24
  111.3 73.3 %all-reduce.2.cloned.1.call-done = f32[512,256]{1,0:T(8,128)} async-done(((f32[512,256]{1,0:T(8,128)}), f32[512,256]{1,0:T(8,128)}) %all-reduce.2.cloned.1.call-update) | async-done | bytes 524304 | tf_op jit(solution)/shard_map/psum | solution.py:35
  184.6 2.1 %sub.3 = f32[512,256]{1,0:T(8,128)} subtract(f32[512,256]{1,0:T(8,128)} %param.6, f32[512,256]{1,0:T(8,128)} %all-reduce.2.cloned.1.call-done) | non-fusion elementwise | flops 131072 | bytes 1572864 | tf_op jit(solution)/shard_map/sub | solution.py:36
  (12 shorter events, 0.1 us)
Async XLA Ops:
  7.2 85.5 %copy-start = (bf16[512,2048]{1,0:T(8,128)(2,1)S(1)}, bf16[512,2048]{1,0:T(8,128)(2,1)}, u32[]{:S(2)}) copy-start(bf16[512,2048]{1,0:T(8,128)(2,1)} %param.4) | copy-start | bytes 6291460
  7.2 85.4 %all-gather.2.cloned.1.call-start = ((), (), s32[]{:S(2)}) async-start(), calls=%async_computation.2 | async-start | bytes 4718592 | tf_op jit(solution)/shard_map/all_gather | solution.py:24
  15.1 91.5 %reduce-scatter.2.cloned.1.call-start = ((), (), s32[]{:S(2)}) async-start(), calls=%async_computation.3 | async-start | bytes 3145728 | tf_op jit(solution)/shard_map/reduce_scatter | solution.py:27
  98.5 1.0 copy-start.1
  98.5 86.0 %all-reduce.2.cloned.1.call-start = ((), (), s32[]{:S(2)}) async-start(), calls=%async_computation.4 | async-start | bytes 1048576 | tf_op jit(solution)/shard_map/psum | solution.py:35
  106.6 1.8 copy-start.2
Sparse Core Ops, SparseCore 0:
  15.2 77.3 all-gather.1
  98.6 7.9 reduce-scatter.1
  110.6 73.9 all-reduce.1
where the time goes:
time: 193 us
  waiting for transfers between devices  155 us (80%)
  between operations  13.8 us (7%)
  matrix products  7.35 us (4%)
  local copies, waits for them, and re-layouts  7.1 us (4%)
  other arithmetic  5.29 us (3%)
  blocking collectives  4.15 us (2%)
    all_gather x1, waiting for transfers between devices, per_device(): lax.all_gather(swapped, 'prow', axis=0, tiled=True)  77.5 us
    psum x1, waiting for transfers between devices, per_device(): totals = lax.psum(diag_terms, 'prow')  73.3 us
    dot_general x1, matrix products, per_device(): jnp.dot(ancestor_inverse, lax.all_gather(swapped, 'prow', axis=0, tiled=T...  5.87 us
    reduce_scatter x1, waiting for transfers between devices, per_device(): lax.psum_scatter(partial_sum, 'pcol', scatter_dimension=1, tiled=True)  4.52 us
    all_to_all x1, blocking collectives, per_device(): lax.all_to_all(masked, 'pcol', split_axis=0, concat_axis=1, tiled=True)  4.15 us
  transfers between devices with their start and end apart: 3, of which 3 were waited for; matrix products, arithmetic and copies ran while one was open for 2% of the time, Pallas kernels for 0%

commit v1 on v0

--- a/solution.py
+++ b/solution.py
@@ -32,7 +32,9 @@
         negated.reshape(-1, local_nodes, B),
         precision=lax.Precision.HIGHEST,
     )
-    totals = lax.psum(diag_terms, "prow")
+    totals = diag_terms
+    for hop in (1, 2, 4):
+        totals = totals + lax.ppermute(totals, "prow", [(dev, dev ^ hop) for dev in range(8)])
     diag_blocks = diag_inverse - totals.reshape(local_nodes * B, B)
     column_blocks = (negated.reshape(local_tiles, B, local_nodes, B) * panel_mask).reshape(
         negated.shape

time: 193 us -> 173 us (0.90)
  waiting for transfers between devices: 155 us -> 127 us
  starting transfers between devices: 0.12 us -> 6.24 us
  other arithmetic: 5.29 us -> 7.31 us
    psum x1 -> x0, waiting for transfers between devices: 73.3 us -> none  [per_device(): totals = lax.psum(diag_terms, 'prow')]
    ppermute x0 -> x3, waiting for transfers between devices: none -> 45 us  [per_device(): lax.ppermute(totals, 'prow', [(dev, dev ^ hop) for dev in range(8)])]
    ppermute x0 -> x3, starting transfers between devices: none -> 6.16 us  [per_device(): lax.ppermute(totals, 'prow', [(dev, dev ^ hop) for dev in range(8)])]
    add x0 -> x3, other arithmetic: none -> 2.2 us  [per_device(): totals + lax.ppermute(totals, 'prow', [(dev, dev ^ hop) for dev in range(...]
  transfers between devices with their start and end apart: 3 -> 5, of which waited for: 3 -> 5; matrix products, arithmetic and copies ran while one was open for 2% -> 2% of each run, Pallas kernels for 0% -> 0%
where the time goes in v1:
time: 173 us
  waiting for transfers between devices  127 us (73%)
  between operations  14.1 us (8%)
  other arithmetic  7.31 us (4%)
  local copies, waits for them, and re-layouts  7.15 us (4%)
  matrix products  6.56 us (4%)
  starting transfers between devices  6.24 us (4%)
  blocking collectives  4.15 us (2%)
    all_gather x1, waiting for transfers between devices, per_device(): lax.all_gather(swapped, 'prow', axis=0, tiled=True)  77.5 us
    ppermute x3, waiting for transfers between devices, per_device(): lax.ppermute(totals, 'prow', [(dev, dev ^ hop) for dev in range(8)])  45 us
    ppermute x3, starting transfers between devices, per_device(): lax.ppermute(totals, 'prow', [(dev, dev ^ hop) for dev in range(8)])  6.16 us
    dot_general x1, matrix products, per_device(): jnp.dot(ancestor_inverse, lax.all_gather(swapped, 'prow', axis=0, tiled=T...  5.87 us
    reduce_scatter x1, waiting for transfers between devices, per_device(): lax.psum_scatter(partial_sum, 'pcol', scatter_dimension=1, tiled=True)  4.52 us
    all_to_all x1, blocking collectives, per_device(): lax.all_to_all(masked, 'pcol', split_axis=0, concat_axis=1, tiled=True)  4.15 us
  transfers between devices with their start and end apart: 5, of which 5 were waited for; matrix products, arithmetic and copies ran while one was open for 2% of the time, Pallas kernels for 0%

profile of v1, /device:TPU:0, one launch (start us, length us, event | category | flops | bytes accessed | tf_op | source)
XLA Modules:
  0.0 172.6 jit_solution(1449604601416536138)
XLA Ops:
  7.2 0.8 constant_dynamic-slice_fusion
  8.3 0.3 mul.39
  8.7 1.2 mul.41
  9.9 4.2 %all_to_all.19 = bf16[2,256,512]{2,1,0:T(8,128)(2,1)S(1)} all-to-all(bf16[2,256,512]{2,1,0:T(8,128)(2,1)S(1)} %bitcast.30), channel_id=1, replica_groups=mesh['pole'=2,'prow'=8,'pcol'=2] {'pcol'}, dimensions={0} | all-to-all | bytes 1048576 | tf_op jit(solution)/shard_map/all_to_all | solution.py:21
  14.1 1.0 copy.19
  15.1 77.5 %all-gather.2.cloned.1.call-done = bf16[2048,1024]{0,1:T(8,128)(2,1)} async-done(((bf16[256,1024]{0,1:T(8,128)(2,1)}), bf16[2048,1024]{0,1:T(8,128)(2,1)}) %all-gather.2.cloned.1.call-update) | async-done | bytes 4194320 | tf_op jit(solution)/shard_map/all_gather | solution.py:24
  92.6 5.9 %convolution_bitcast_fusion = f32[512,1024]{0,1:T(8,128)} fusion(bf16[2048,1024]{0,1:T(8,128)(2,1)} %all-gather.2.cloned.1.call-done, bf16[512,2048]{1,0:T(8,128)(2,1)S(1)} %copy-done), kind=kOutput, calls=%fused_computation | convolution fusion | flops 2147483648 | bytes 8388608 | tf_op jit(solution)/shard_map/dot_general | solution.py:22
  98.6 0.9 copy-done.1
  99.5 1.0 copy.26
  100.6 0.3 mul.42
  101.0 1.0 copy.28
  102.1 4.5 %reduce-scatter.2.cloned.1.call-done = f32[512,512]{0,1:T(8,128)} async-done(((f32[512,1024]{0,1:T(8,128)}), f32[512,512]{0,1:T(8,128)}) %reduce-scatter.2.cloned.1.call-update) | async-done | bytes 1048592 | tf_op jit(solution)/shard_map/reduce_scatter | solution.py:27
  106.6 1.8 %fusion.3 = (f32[512,512]{0,1:T(8,128)S(1)}, f32[512,512]{0,1:T(8,128)S(1)}) fusion(f32[512,512]{0,1:T(8,128)} %reduce-scatter.2.cloned.1.call-done, f32[512,512]{0,1:T(8,128)} %bitcast.27), kind=kLoop, calls=%fused_computation.11 | loop fusion | flops 524288 | bytes 4194304 | tf_op jit(solution)/shard_map/neg | solution.py:28
  108.5 0.7 fusion
  109.2 2.0 %collective-permute-start = (f32[2,256,256]{2,1,0:T(8,128)S(1)}, f32[2,256,256]{2,1,0:T(8,128)S(1)}, u32[]{:S(2)}, u32[]{:S(2)}) collective-permute-start(f32[2,256,256]{2,1,0:T(8,128)S(1)} %fusion), channel_id=1, source_target_pairs={{0,2},{2,0},{4,6},{6,4},{8,10},{10,8},{12,14},{14,12},{1,3},{3,1},... | collective-permute-start | bytes 1572872 | tf_op jit(solution)/shard_map/ppermute | solution.py:37
  111.1 12.3 %collective-permute-done = f32[2,256,256]{2,1,0:T(8,128)S(1)} collective-permute-done((f32[2,256,256]{2,1,0:T(8,128)S(1)}, f32[2,256,256]{2,1,0:T(8,128)S(1)}, u32[]{:S(2)}, u32[]{:S(2)}) %collective-permute-start) | collective-permute-done | bytes 524320 | tf_op jit(solution)/shard_map/ppermute | solution.py:37
  123.5 1.7 %collective-permute-start.1 = (f32[2,256,256]{2,1,0:T(8,128)S(1)}, f32[2,256,256]{2,1,0:T(8,128)S(1)}, u32[]{:S(2)}, u32[]{:S(2)}) collective-permute-start(f32[2,256,256]{2,1,0:T(8,128)S(1)} %add.27), channel_id=1, source_target_pairs={{0,4},{2,6},{4,0},{6,2},{8,12},{10,14},{12,8},{14,10},{1,5},{3,7},... | collective-permute-start | bytes 1572872 | tf_op jit(solution)/shard_map/ppermute | solution.py:37
  125.2 11.6 %collective-permute-done.1 = f32[2,256,256]{2,1,0:T(8,128)S(1)} collective-permute-done((f32[2,256,256]{2,1,0:T(8,128)S(1)}, f32[2,256,256]{2,1,0:T(8,128)S(1)}, u32[]{:S(2)}, u32[]{:S(2)}) %collective-permute-start.1) | collective-permute-done | bytes 524320 | tf_op jit(solution)/shard_map/ppermute | solution.py:37
  136.8 0.9 add.28
  137.7 2.5 %collective-permute-start.2 = (f32[2,256,256]{2,1,0:T(8,128)}, f32[2,256,256]{2,1,0:T(8,128)}, u32[]{:S(2)}, u32[]{:S(2)}) collective-permute-start(f32[2,256,256]{2,1,0:T(8,128)} %add.28), channel_id=1, source_target_pairs={{0,8},{2,10},{4,12},{6,14},{8,0},{10,2},{12,4},{14,6},{1,9},{3,11}... | collective-permute-start | bytes 1572872 | tf_op jit(solution)/shard_map/ppermute | solution.py:37
  140.1 1.3 copy.24
  141.4 21.1 %collective-permute-done.2 = f32[2,256,256]{2,1,0:T(8,128)} collective-permute-done((f32[2,256,256]{2,1,0:T(8,128)}, f32[2,256,256]{2,1,0:T(8,128)}, u32[]{:S(2)}, u32[]{:S(2)}) %collective-permute-start.2) | collective-permute-done | bytes 524320 | tf_op jit(solution)/shard_map/ppermute | solution.py:37
  162.6 1.3 add.29
  163.8 1.9 %bitcast_subtract_fusion = f32[512,256]{1,0:T(8,128)} fusion(f32[512,256]{1,0:T(8,128)} %param.6, f32[2,256,256]{2,1,0:T(8,128)S(1)} %add.29), kind=kLoop, calls=%fused_computation.1 | loop fusion | flops 131072 | bytes 1572864 | tf_op jit(solution)/shard_map/sub | solution.py:38
  (18 shorter events, 0.8 us)
Async XLA Ops:
  7.2 85.5 %copy-start = (bf16[512,2048]{1,0:T(8,128)(2,1)S(1)}, bf16[512,2048]{1,0:T(8,128)(2,1)}, u32[]{:S(2)}) copy-start(bf16[512,2048]{1,0:T(8,128)(2,1)} %param.4) | copy-start | bytes 6291460
  7.2 85.4 %all-gather.2.cloned.1.call-start = ((), (), s32[]{:S(2)}) async-start(), calls=%async_computation.2 | async-start | bytes 4718592 | tf_op jit(solution)/shard_map/all_gather | solution.py:24
  15.1 91.5 %reduce-scatter.2.cloned.1.call-start = ((), (), s32[]{:S(2)}) async-start(), calls=%async_computation.3 | async-start | bytes 3145728 | tf_op jit(solution)/shard_map/reduce_scatter | solution.py:27
  98.5 1.0 copy-start.1
  106.6 1.8 %copy-start.2 = (bf16[512,512]{0,1:T(8,128)(2,1)S(1)}, bf16[512,512]{0,1:T(8,128)(2,1)}, u32[]{:S(2)}) copy-start(bf16[512,512]{0,1:T(8,128)(2,1)} %copy.26) | copy-start | bytes 1572868
  109.2 14.2 %collective-permute-start = (f32[2,256,256]{2,1,0:T(8,128)S(1)}, f32[2,256,256]{2,1,0:T(8,128)S(1)}, u32[]{:S(2)}, u32[]{:S(2)}) collective-permute-start(f32[2,256,256]{2,1,0:T(8,128)S(1)} %fusion), channel_id=1, source_target_pairs={{0,2},{2,0},{4,6},{6,4},{8,10},{10,8},{12,14},{14,12},{1,3},{3,1},... | collective-permute-start | bytes 1572872 | tf_op jit(solution)/shard_map/ppermute | solution.py:37
  123.5 13.4 %collective-permute-start.1 = (f32[2,256,256]{2,1,0:T(8,128)S(1)}, f32[2,256,256]{2,1,0:T(8,128)S(1)}, u32[]{:S(2)}, u32[]{:S(2)}) collective-permute-start(f32[2,256,256]{2,1,0:T(8,128)S(1)} %add.27), channel_id=1, source_target_pairs={{0,4},{2,6},{4,0},{6,2},{8,12},{10,14},{12,8},{14,10},{1,5},{3,7},... | collective-permute-start | bytes 1572872 | tf_op jit(solution)/shard_map/ppermute | solution.py:37
  137.7 24.9 %collective-permute-start.2 = (f32[2,256,256]{2,1,0:T(8,128)}, f32[2,256,256]{2,1,0:T(8,128)}, u32[]{:S(2)}, u32[]{:S(2)}) collective-permute-start(f32[2,256,256]{2,1,0:T(8,128)} %add.28), channel_id=1, source_target_pairs={{0,8},{2,10},{4,12},{6,14},{8,0},{10,2},{12,4},{14,6},{1,9},{3,11}... | collective-permute-start | bytes 1572872 | tf_op jit(solution)/shard_map/ppermute | solution.py:37
Sparse Core Ops, SparseCore 0:
  15.2 77.3 all-gather.1
  98.6 7.9 reduce-scatter.1
